TPU v7x, 512 devices: a whole 4x8x8 slice. The times are simulated.
512 devices in a mesh: shot: 16 (over y, core), brick: 32 (over x, z).
Axes of the slice: x: 4, y: 8, z: 8, core: 2. Of those that a mesh axis runs over, the one named last changes fastest.
Arguments:
- pressure: float32 [128, 1024, 512], P('shot', 'brick'), may hold values from -6 to 6
- auxiliary: float32 [128, 1024, 512], P('shot', 'brick'), may hold values from -6 to 6
- pressure_prior: float32 [128, 1024, 512], P('shot', 'brick'), may hold values from -6 to 6
- auxiliary_prior: float32 [128, 1024, 512], P('shot', 'brick'), may hold values from -6 to 6
- courant_sq: float32 [1024, 512], P('brick'), may hold values from 0.05 to 0.2
- thomsen_epsilon: float32 [1024, 512], P('brick'), may hold values from 0.1 to 0.35
- thomsen_delta: float32 [1024, 512], P('brick'), may hold values from 0 to 0.1
- tilt_angle: float32 [1024, 512], P('brick'), may hold values from -3.140625 to 3.140625
- frequencies: float32 [16], replicated, may hold values from 0.05 to 1.5
- spectra: float32 [128, 32, 16384], P('shot', None, 'brick'), may hold values from -6 to 6
- target_cells: int32 [16384], P('brick'), may hold values from 0 to 16383, as said below
- patch_lists: int32 [32, 16, 3, 128], P('brick'), may hold values from 0 to 511, as said below
- patch_counts: int32 [32, 16], P('brick', 'shot'), may hold values from 1 to 3, as said below
Outputs:
- pressure_out: float32 [128, 1024, 512], P('shot', 'brick')
- auxiliary_out: float32 [128, 1024, 512], P('shot', 'brick')
- spectra_out: float32 [128, 32, 16384], P('shot', None, 'brick')
- gram_tiles: float32 [32, 16, 3, 128, 128], P('brick', 'shot')
Inputs may be any that keep to these rules, and one draw needn't show every extreme that they name: `target_cells`: the block of each brick holds distinct cells of that brick. `patch_lists`: target numbers within the owner's brick; the cells of one patch slot are distinct. `patch_counts`: in every brick some owner has all 3 slots live.
All inputs are finite; a program needn't handle non-finite values.
Results may differ from a plain program's by a relative error of at most 0.00077.
Values may be sent and summed in bfloat16 or wider, within the bound.
A program may use at most 64 MiB of HBM per device.

v0:
```python
import jax
import jax.numpy as jnp
from jax import lax
from jax.sharding import PartitionSpec as P

STEPS = 4
PATCH = 128
P_MAX = 3


def with_halo(cells, sides, width):
    for axis, dim in sides:
        count = lax.axis_size(axis)
        ends = count - 1
        head = lax.slice_in_dim(cells, 0, width, axis=dim)
        tail = lax.slice_in_dim(cells, cells.shape[dim] - width, cells.shape[dim], axis=dim)
        cells = jnp.concatenate(
            [
                lax.ppermute(tail, axis, [(i, (i + 1) % count) for i in range(ends)]),
                cells,
                lax.ppermute(head, axis, [((i + 1) % count, i) for i in range(ends)]),
            ],
            axis=dim,
        )
    return cells


def tilt_terms(tilt_angle):
    sine = jnp.sin(tilt_angle)
    cosine = jnp.cos(tilt_angle)
    return (sine * sine, cosine * cosine, 2.0 * sine * cosine)


def derivatives(field, sine_sq, cosine_sq, double_sin):
    widths = [(0, 0)] * (field.ndim - 1) + [(1, 1)]
    padded = jnp.pad(field, widths)
    centre = padded[..., 1:-1, 1:-1]
    second_x = padded[..., 2:, 1:-1] - 2.0 * centre + padded[..., :-2, 1:-1]
    second_z = padded[..., 1:-1, 2:] - 2.0 * centre + padded[..., 1:-1, :-2]
    mixed = 0.25 * (
        padded[..., 2:, 2:] - padded[..., 2:, :-2] - padded[..., :-2, 2:] + padded[..., :-2, :-2]
    )
    along_axis = sine_sq * second_x + cosine_sq * second_z + double_sin * mixed
    across_axis = second_x + second_z - along_axis
    return (along_axis, across_axis)


def leapfrog(extended, former, coefficients):
    courant_sq, epsilon, delta_value, sine_sq, cosine_sq, double_sin = coefficients
    along_p, across_p = derivatives(extended[0], sine_sq, cosine_sq, double_sin)
    along_q, across_q = derivatives(extended[1], sine_sq, cosine_sq, double_sin)
    pressure = extended[0][..., 1:-1, :]
    auxiliary = extended[1][..., 1:-1, :]
    pressure_next = (
        2.0 * pressure - former[0] + courant_sq * ((1.0 + 2.0 * epsilon) * across_p + along_q)
    )
    auxiliary_next = (
        2.0 * auxiliary - former[1] + courant_sq * ((1.0 + 2.0 * delta_value) * across_p + along_q)
    )
    return jnp.stack([pressure_next, auxiliary_next])


def shards(
    pressure,
    auxiliary,
    pressure_prior,
    auxiliary_prior,
    courant_sq,
    thomsen_epsilon,
    thomsen_delta,
    tilt_angle,
    frequencies,
    spectra,
    target_cells,
    patch_lists,
    patch_counts,
):
    shots_here, width_x, depth = pressure.shape
    samples = []
    packed = jnp.concatenate(
        [
            jnp.stack([pressure, auxiliary, pressure_prior, auxiliary_prior]).reshape(
                4 * shots_here, width_x, depth
            ),
            jnp.stack([courant_sq, thomsen_epsilon, thomsen_delta, tilt_angle]),
        ],
        0,
    )
    widened = with_halo(packed, (("brick", 1),), STEPS)
    states = widened[: 4 * shots_here].reshape(4, shots_here, width_x + 2 * STEPS, depth)
    params = widened[4 * shots_here :]
    sine_sq, cosine_sq, double_sin = tilt_terms(params[3])
    full_coefficients = (params[0], params[1], params[2], sine_sq, cosine_sq, double_sin)
    current = states[:2]
    former = states[2:]
    for moment in range(STEPS):
        trimmed = moment + 1
        coefficients = tuple(
            (item[trimmed : item.shape[0] - trimmed] for item in full_coefficients)
        )
        advanced = leapfrog(current, former[:, :, 1:-1], coefficients)
        former = current[:, :, 1:-1]
        current = advanced
        margin = STEPS - moment - 1
        interior = current[0][:, margin : margin + width_x]
        samples.append(
            jnp.take(interior.reshape(shots_here, width_x * depth), target_cells, axis=1)
        )
    spectra_out = spectra
    for moment in range(STEPS):
        angle = frequencies * (moment + 1.0)
        table = jnp.concatenate([jnp.cos(angle), -jnp.sin(angle)])
        spectra_out = spectra_out + table[None, :, None] * samples[moment][:, None, :]
    local_features = spectra_out.shape[0] * spectra_out.shape[1]
    features = spectra_out.reshape(local_features, spectra_out.shape[2]).astype(jnp.bfloat16)
    owners = patch_lists.shape[1]
    total_features = local_features * owners
    live_slots = (jnp.arange(P_MAX, dtype=jnp.int32) < patch_counts[0, 0]).astype(jnp.float32)
    own_lists = lax.dynamic_index_in_dim(
        patch_lists[0], lax.axis_index("shot"), 0, keepdims=False
    ).reshape(-1)
    portion = lax.all_gather(features, "shot", axis=0, tiled=True)
    selected = jnp.take(portion, own_lists, axis=1).reshape(portion.shape[0], P_MAX, PATCH)
    grams = jnp.einsum("fpa,fpb->pab", selected, selected, preferred_element_type=jnp.float32)
    gram_tiles = grams / total_features * live_slots[:, None, None]
    return (current[0], current[1], spectra_out, gram_tiles.reshape(1, 1, P_MAX, PATCH, PATCH))


def solution(mesh):
    return jax.shard_map(
        shards,
        mesh=mesh,
        in_specs=(
            P("shot", "brick", None),
            P("shot", "brick", None),
            P("shot", "brick", None),
            P("shot", "brick", None),
            P("brick", None),
            P("brick", None),
            P("brick", None),
            P("brick", None),
            P(),
            P("shot", None, "brick"),
            P("brick"),
            P("brick", None, None, None),
            P("brick", "shot"),
        ),
        out_specs=(
            P("shot", "brick", None),
            P("shot", "brick", None),
            P("shot", None, "brick"),
            P("brick", "shot", None, None, None),
        ),
        check_vma=False,
    )
```

profile of v0, /device:TPU:1, one launch (start us, length us, event | category | flops | bytes accessed | tf_op | source)
XLA Modules:
  0.0 157.3 jit_solution(15979312028043918637)
XLA Ops:
  7.2 1.7 %pad_maximum_fusion.1 = f32[4,8,32,512]{3,2,1,0:T(8,128)S(1)} fusion(f32[1,8,32,512]{3,2,1,0:T(8,128)} %bitcast.150, f32[1,8,32,512]{3,2,1,0:T(8,128)} %bitcast.151, f32[1,8,32,512]{3,2,1,0:T(8,128)} %bitcast.152, f32[1,8,32,512]{3,2,1,0:T(8,128)} %bitcast.153), kind=kLoop, calls=%fused_computation.9 | loop fusion | flops 1572864 | bytes 4194304 | tf_op jit(solution)/shard_map/stack | solution.py:82
  9.2 0.6 copy-done.1
  10.0 4.8 %collective-permute-start = (f32[36,4,512]{2,1,0:T(4,128)S(1)}, f32[36,4,512]{2,1,0:T(4,128)S(1)}, u32[]{:S(2)}, u32[]{:S(2)}) collective-permute-start(f32[36,4,512]{2,1,0:T(4,128)S(1)} %get-tuple-element.36), channel_id=1, source_target_pairs={{0,1},{1,2},{2,3},{3,4},{4,5},{5,6},{6,7},{7,8},{8,9},{9,10},{10,1... | collective-permute-start | bytes 884744 | tf_op jit(solution)/shard_map/ppermute | solution.py:19
  14.8 1.3 collective-permute-start.1
  16.5 2.0 %collective-permute-done = f32[36,4,512]{2,1,0:T(4,128)S(1)} collective-permute-done((f32[36,4,512]{2,1,0:T(4,128)S(1)}, f32[36,4,512]{2,1,0:T(4,128)S(1)}, u32[]{:S(2)}, u32[]{:S(2)}) %collective-permute-start) | collective-permute-done | bytes 294944 | tf_op jit(solution)/shard_map/ppermute | solution.py:19
  18.5 4.8 %collective-permute-done.1 = f32[36,4,512]{2,1,0:T(4,128)S(1)} collective-permute-done((f32[36,4,512]{2,1,0:T(4,128)S(1)}, f32[36,4,512]{2,1,0:T(4,128)S(1)}, u32[]{:S(2)}, u32[]{:S(2)}) %collective-permute-start.1) | collective-permute-done | bytes 294944 | tf_op jit(solution)/shard_map/ppermute | solution.py:21
  23.2 0.3 fusion.125
  23.5 0.3 multiply_multiply_fusion
  23.9 0.4 pad_maximum_fusion
  24.5 0.3 fusion.127
  24.8 2.3 %fusion.75 = (f32[8,38,512]{2,1,0:T(8,128)S(1)}, f32[8,38,512]{2,1,0:T(8,128)S(1)}, f32[8,38,512]{2,1,0:T(8,128)S(1)}) fusion(f32[2,8,40,512]{3,2,1,0:T(8,128)S(1)} %bitcast.146, f32[36,40,512]{2,1,0:T(8,128)S(1)} %pad_maximum_fusion, f32[38,512]{1,0:T(8,128)S(1)} %get-tuple-element.30, f32[38,512]{1,0:T(8,128)S(1)} %get-tuple-element.31, ...), kind=kLoop, calls=%fused_computation.149 | loop fusion | flops 5136384 | bytes 7925760 | tf_op jit(solution)/shard_map/add | solution.py:55
  27.2 0.3 fusion.70
  27.6 2.3 %fusion.65 = (f32[8,36,512]{2,1,0:T(8,128)S(1)}, f32[8,36,512]{2,1,0:T(8,128)S(1)}, f32[8,36,512]{2,1,0:T(8,128)S(1)}) fusion(f32[2,8,40,512]{3,2,1,0:T(8,128)S(1)} %bitcast.144, f32[8,38,512]{2,1,0:T(8,128)S(1)} %fusion.70, f32[36,512]{1,0:T(8,128)S(1)} %get-tuple-element.27, f32[36,512]{1,0:T(8,128)S(1)} %get-tuple-element.28, ...), kind=kLoop, calls=%fused_computation.121 | loop fusion | flops 4866048 | bytes 8077312 | tf_op jit(solution)/shard_map/add | solution.py:58
  29.9 0.3 fusion.72
  30.3 2.3 %fusion.67 = (f32[8,34,512]{2,1,0:T(8,128)S(1)}, f32[8,34,512]{2,1,0:T(8,128)S(1)}, f32[8,34,512]{2,1,0:T(8,128)S(1)}) fusion(f32[1,8,38,512]{3,2,1,0:T(8,128)S(1)} %bitcast.135, f32[8,36,512]{2,1,0:T(8,128)S(1)} %fusion.72, f32[34,512]{1,0:T(8,128)S(1)} %get-tuple-element.24, f32[34,512]{1,0:T(8,128)S(1)} %get-tuple-element.25, ...), kind=kLoop, calls=%fused_computation.126 | loop fusion | flops 4595712 | bytes 7979008 | tf_op jit(solution)/shard_map/add | solution.py:55
  32.6 0.3 fusion.62
  33.0 2.6 %fusion.94 = (f32[8,32,512]{2,1,0:T(8,128)}, f32[8,32,512]{2,1,0:T(8,128)S(1)}, f32[8,32,512]{2,1,0:T(8,128)S(1)}) fusion(f32[1,8,36,512]{3,2,1,0:T(8,128)S(1)} %bitcast.136, f32[8,34,512]{2,1,0:T(8,128)S(1)} %fusion.62, f32[32,512]{1,0:T(8,128)S(1)} %multiply_add_fusion.1, f32[32,512]{1,0:T(8,128)S(1)} %copy-done.1, f32[32,512]{1,0:T(8,128)S(1)} %get-tuple-element.61, ...), kind=kLoop, calls=%fused_computation.170 | loop fusion | flops 4325376 | bytes 6881280 | tf_op jit(solution)/shard_map/add | solution.py:58
  35.5 0.5 fusion.129
  36.0 4.6 %copy.31 = f32[8,32,512]{0,2,1:T(8,128)} copy(f32[8,32,512]{2,1,0:T(8,128)S(1)} %get-tuple-element.38) | data formatting | bytes 1048576 | tf_op jit(solution)/shard_map/slice | solution.py:52
  40.7 4.7 %copy.29 = f32[8,32,512]{0,2,1:T(8,128)} copy(f32[8,32,512]{2,1,0:T(8,128)S(1)} %slice.655) | data formatting | bytes 1048576 | tf_op jit(solution)/shard_map/slice | solution.py:105
  45.3 4.4 %gather_fusion.3 = f32[512,8]{1,0:T(8,128)S(1)} fusion(f32[8,16384]{0,1:T(8,128)} %bitcast.139, s32[1024]{0:T(1024)S(1)} %pad_clamp_fusion.1), kind=kCustom, calls=%fused_computation.2.clone | custom fusion | bytes 34816 | tf_op jit(solution)/shard_map/jit(_take)/gather | solution.py:107
  49.7 4.4 %gather_fusion.2 = f32[512,8]{1,0:T(8,128)S(1)} fusion(f32[8,16384]{0,1:T(8,128)} %bitcast.140, s32[1024]{0:T(1024)S(1)} %pad_clamp_fusion.1), kind=kCustom, calls=%fused_computation.1.clone | custom fusion | bytes 34816 | tf_op jit(solution)/shard_map/jit(_take)/gather | solution.py:107
  54.1 4.7 %copy.27 = f32[8,32,512]{0,2,1:T(8,128)} copy(f32[8,32,512]{2,1,0:T(8,128)S(1)} %slice.654) | data formatting | bytes 1048576 | tf_op jit(solution)/shard_map/slice | solution.py:105
  58.8 4.4 %gather_fusion.1 = f32[512,8]{1,0:T(8,128)S(1)} fusion(f32[8,16384]{0,1:T(8,128)} %bitcast.141, s32[1024]{0:T(1024)S(1)} %pad_clamp_fusion.1), kind=kCustom, calls=%fused_computation.clone | custom fusion | bytes 34816 | tf_op jit(solution)/shard_map/jit(_take)/gather | solution.py:107
  63.2 4.7 %copy.33 = f32[8,32,512]{0,2,1:T(8,128)} copy(f32[8,32,512]{2,1,0:T(8,128)S(1)} %get-tuple-element.39) | data formatting | bytes 1048576 | tf_op jit(solution)/shard_map/add | solution.py:55
  67.9 4.5 %gather_fusion.4 = f32[512,8]{1,0:T(8,128)S(1)} fusion(f32[8,16384]{0,1:T(8,128)} %bitcast.142, s32[1024]{0:T(1024)S(1)} %pad_clamp_fusion.1), kind=kCustom, calls=%fused_computation.3.clone | custom fusion | bytes 34816 | tf_op jit(solution)/shard_map/jit(_take)/gather | solution.py:107
  72.9 1.0 fusion.116
  74.0 0.8 copy.35
  75.5 0.7 fusion.114
  76.2 58.6 %all-gather.2.cloned.1.call-done = bf16[4096,512]{0,1:T(8,128)(2,1)} async-done(((bf16[256,512]{0,1:T(8,128)(2,1)}), bf16[4096,512]{0,1:T(8,128)(2,1)}) %all-gather.2.cloned.1.call-update) | async-done | bytes 4194320 | tf_op jit(solution)/shard_map/all_gather | solution.py:122
  134.8 10.9 %gather_fusion = bf16[384,4096]{1,0:T(8,128)(2,1)} fusion(bf16[4096,512]{0,1:T(8,128)(2,1)} %all-gather.2.cloned.1.call-done, s32[1024]{0:T(1024)S(1)} %pad_clamp_fusion), kind=kCustom, calls=%fused_computation.4 | custom fusion | bytes 6292992 | tf_op jit(solution)/shard_map/jit(_take)/gather | solution.py:123
  145.8 4.6 %fusion.7 = f32[1,1,3,128,128]{4,3,2,1,0:T(8,128)} fusion(bf16[4096,3,128]{0,2,1:T(8,128)(2,1)} %bitcast.148, pred[3,128]{1,0:T(4,128)(4,1)S(1)} %compare_and_fusion.1, f32[3]{0:T(128)S(1)} %compare_select_fusion.3), kind=kOutput, calls=%fused_computation.12 | convolution fusion | flops 404275200 | bytes 3342732 | tf_op jit(solution)/shard_map/fpa,fpb->pab/dot_general | solution.py:124
  (50 shorter events, 1.8 us)
Async XLA Ops:
  7.2 127.7 %all-gather.2.cloned.1.call-start = ((), (), s32[]{:S(2)}) async-start(), calls=%async_computation | async-start | bytes 4456448 | tf_op jit(solution)/shard_map/all_gather | solution.py:122
  8.9 0.8 copy-start.1
  8.9 0.9 copy-start.3
  8.9 0.9 copy-start.4
  9.0 0.9 copy-start.5
  9.0 7.2 %copy-start.6 = (s32[512]{0:T(512)S(1)}, s32[512]{0:T(512)}, u32[]{:S(2)}) copy-start(s32[512]{0:T(512)} %param.25) | copy-start | bytes 6148
  9.0 7.2 %copy-start.7 = (f32[16]{0:T(128)S(1)}, f32[16]{0:T(128)}, u32[]{:S(2)}) copy-start(f32[16]{0:T(128)} %param.23) | copy-start | bytes 196
  10.0 8.5 %collective-permute-start = (f32[36,4,512]{2,1,0:T(4,128)S(1)}, f32[36,4,512]{2,1,0:T(4,128)S(1)}, u32[]{:S(2)}, u32[]{:S(2)}) collective-permute-start(f32[36,4,512]{2,1,0:T(4,128)S(1)} %get-tuple-element.36), channel_id=1, source_target_pairs={{0,1},{1,2},{2,3},{3,4},{4,5},{5,6},{6,7},{7,8},{8,9},{9,10},{10,1... | collective-permute-start | bytes 884744 | tf_op jit(solution)/shard_map/ppermute | solution.py:19
  14.8 8.4 %collective-permute-start.1 = (f32[36,4,512]{2,1,0:T(4,128)S(1)}, f32[36,4,512]{2,1,0:T(4,128)S(1)}, u32[]{:S(2)}, u32[]{:S(2)}) collective-permute-start(f32[36,4,512]{2,1,0:T(4,128)S(1)} %get-tuple-element.37), channel_id=1, source_target_pairs={{1,0},{2,1},{3,2},{4,3},{5,4},{6,5},{7,6},{8,7},{9,8},{10,9},{11,1... | collective-permute-start | bytes 884744 | tf_op jit(solution)/shard_map/ppermute | solution.py:21
  36.0 27.2 %copy-start = (f32[8,32,512]{2,1,0:T(8,128)}, f32[8,32,512]{2,1,0:T(8,128)S(1)}, u32[]{:S(2)}) copy-start(f32[8,32,512]{2,1,0:T(8,128)S(1)} %get-tuple-element.39) | copy-start | bytes 1572868
  67.9 5.0 %copy-start.2 = (f32[8,32,512]{2,1,0:T(8,128)S(1)}, f32[8,32,512]{2,1,0:T(8,128)}, u32[]{:S(2)}) copy-start(f32[8,32,512]{2,1,0:T(8,128)} %param.24) | copy-start | bytes 1572868
Sparse Core Ops, SparseCore 0:
  74.9 59.8 all-gather.1
where the time goes:
time: 158 us; the launch traced here: 157 us
  waiting for transfers between devices  65.4 us (41%)
  local copies, waits for them, and re-layouts  50 us (32%)
  other arithmetic  16 us (10%)
  between operations  15.1 us (10%)
  starting transfers between devices  6.16 us (4%)
  matrix products  4.63 us (3%)
    all_gather x1, waiting for transfers between devices, shards(): portion = lax.all_gather(features, 'shot', axis=0, tiled=True)  58.6 us
    gather x4, local copies, waits for them, and re-layouts, shards(): jnp.take(interior.reshape(shots_here, width_x * depth), target_cells, axi...  17.7 us
    gather x1, local copies, waits for them, and re-layouts, shards(): jnp.take(portion, own_lists, axis=1).reshape(portion.shape[0], P_MAX, PATCH)  10.9 us
    slice x4, local copies, waits for them, and re-layouts, shards(): interior = current[0][:, margin:margin + width_x]  9.44 us
    add x4, other arithmetic, leapfrog(): 2.0 * auxiliary - former[1]  5.53 us
    add x3, other arithmetic, leapfrog(): 2.0 * pressure - former[0]  4.87 us
    ppermute x1, starting transfers between devices, with_halo(): lax.ppermute(tail, axis, [(i, (i + 1) % count) for i in range(ends)])  4.83 us
    ppermute x1, waiting for transfers between devices, with_halo(): lax.ppermute(head, axis, [((i + 1) % count, i) for i in range(ends)])  4.76 us
  transfers between devices with their start and end apart: 3, of which 3 were waited for; matrix products, arithmetic and copies ran while one was open for 1% of the time, Pallas kernels for 0%

commit v1 on v0

--- a/solution.py
+++ b/solution.py
@@ -119,7 +119,16 @@
     own_lists = lax.dynamic_index_in_dim(
         patch_lists[0], lax.axis_index("shot"), 0, keepdims=False
     ).reshape(-1)
-    portion = lax.all_gather(features, "shot", axis=0, tiled=True)
+    ways = lax.axis_size("shot")
+    up = [(d, (d + 1) % ways) for d in range(ways)]
+    down = [(d, (d - 1) % ways) for d in range(ways)]
+    earlier, later = ([features], [features])
+    for _ in range(ways // 2):
+        earlier.append(lax.ppermute(earlier[-1], "shot", up))
+    for _ in range((ways - 1) // 2):
+        later.append(lax.ppermute(later[-1], "shot", down))
+    line = jnp.concatenate([*earlier[::-1], *later[1:]], axis=0)
+    portion = jnp.roll(line, (lax.axis_index("shot") - ways // 2) * features.shape[0], axis=0)
     selected = jnp.take(portion, own_lists, axis=1).reshape(portion.shape[0], P_MAX, PATCH)
     grams = jnp.einsum("fpa,fpb->pab", selected, selected, preferred_element_type=jnp.float32)
     gram_tiles = grams / total_features * live_slots[:, None, None]

time: 158 us -> 180 us (1.14)
  the two profiles are of different devices: /device:TPU:1 before, /device:TPU:31 now
where the time goes in v1:
time: 180 us; the launch traced here: 179 us
  local copies, waits for them, and re-layouts  63.5 us (35%)
  starting transfers between devices  43 us (24%)
  waiting for transfers between devices  35.2 us (20%)
  other arithmetic  33.6 us (19%)
  between operations  1.98 us (1%)
    ppermute x8, starting transfers between devices, shards(): earlier.append(lax.ppermute(earlier[-1], 'shot', up))  30.2 us
    ppermute x8, waiting for transfers between devices, shards(): earlier.append(lax.ppermute(earlier[-1], 'shot', up))  24.1 us
    gather x4, local copies, waits for them, and re-layouts, shards(): jnp.take(interior.reshape(shots_here, width_x * depth), target_cells, axi...  19.1 us
    slice x4, local copies, waits for them, and re-layouts, shards(): interior = current[0][:, margin:margin + width_x]  13.4 us
    add x3, other arithmetic, leapfrog(): 2.0 * pressure - former[0]  11.8 us
    ppermute x1, starting transfers between devices, with_halo(): lax.ppermute(head, axis, [((i + 1) % count, i) for i in range(ends)])  10.9 us
    add x4, other arithmetic, leapfrog(): 2.0 * auxiliary - former[1]  10.2 us
    gather x1, local copies, waits for them, and re-layouts, shards(): jnp.take(portion, own_lists, axis=1).reshape(portion.shape[0], P_MAX, PATCH)  10.2 us
  transfers between devices with their start and end apart: 17, of which 12 were waited for; matrix products, arithmetic and copies ran while one was open for 3% of the time, Pallas kernels for 0%

profile of v1, /device:TPU:31, one launch (start us, length us, event | category | flops | bytes accessed | tf_op | source)
XLA Modules:
  0.0 179.1 jit_solution(7288092853173535500)
XLA Ops:
  3.0 10.9 %collective-permute-start.1 = (f32[36,4,512]{2,1,0:T(4,128)S(1)}, f32[36,4,512]{2,1,0:T(4,128)S(1)}, u32[]{:S(2)}, u32[]{:S(2)}) collective-permute-start(f32[36,4,512]{2,1,0:T(4,128)S(1)} %get-tuple-element.37), channel_id=1, source_target_pairs={{1,0},{2,1},{3,2},{4,3},{5,4},{6,5},{7,6},{8,7},{9,8},{10,9},{11,1... | collective-permute-start | bytes 884744 | tf_op jit(solution)/shard_map/ppermute | solution.py:21
  19.6 5.9 %collective-permute-done = f32[36,4,512]{2,1,0:T(4,128)S(1)} collective-permute-done((f32[36,4,512]{2,1,0:T(4,128)S(1)}, f32[36,4,512]{2,1,0:T(4,128)S(1)}, u32[]{:S(2)}, u32[]{:S(2)}) %collective-permute-start) | collective-permute-done | bytes 294944 | tf_op jit(solution)/shard_map/ppermute | solution.py:19
  31.7 3.3 %fusion.75 = (f32[8,38,512]{2,1,0:T(8,128)S(1)}, f32[8,38,512]{2,1,0:T(8,128)}, f32[8,38,512]{2,1,0:T(8,128)}) fusion(f32[2,8,40,512]{3,2,1,0:T(8,128)S(1)} %bitcast.146, f32[36,40,512]{2,1,0:T(8,128)S(1)} %pad_maximum_fusion, f32[38,512]{1,0:T(8,128)S(1)} %get-tuple-element.30, f32[38,512]{1,0:T(8,128)S(1)} %get-tuple-element.31, ...), kind=kLoop, calls=%fused_computation.149 | loop fusion | flops 5136384 | bytes 7925760 | tf_op jit(solution)/shard_map/add | solution.py:55
  35.8 5.9 %copy.27 = f32[8,32,512]{0,2,1:T(8,128)} copy(f32[8,32,512]{2,1,0:T(8,128)} %slice.654) | data formatting | bytes 1048576 | tf_op jit(solution)/shard_map/slice | solution.py:105
  44.7 4.2 %fusion.65 = (f32[8,36,512]{2,1,0:T(8,128)}, f32[8,36,512]{2,1,0:T(8,128)S(1)}, f32[8,36,512]{2,1,0:T(8,128)S(1)}) fusion(f32[2,8,40,512]{3,2,1,0:T(8,128)} %bitcast.144, f32[8,38,512]{2,1,0:T(8,128)S(1)} %fusion.70, f32[36,512]{1,0:T(8,128)S(1)} %get-tuple-element.27, f32[36,512]{1,0:T(8,128)S(1)} %get-tuple-element.28, f32[36,512]{1,0:T(8,128)} %get-tuple-element.57, ...), kind=kLoop, calls=%fused_computation.121 | loop fusion | flops 4866048 | bytes 7995392 | tf_op jit(solution)/shard_map/add | solution.py:58
  51.0 5.8 %copy.29 = f32[8,32,512]{0,2,1:T(8,128)} copy(f32[8,32,512]{2,1,0:T(8,128)} %slice.655) | data formatting | bytes 1048576 | tf_op jit(solution)/shard_map/slice | solution.py:105
  56.8 5.0 %gather_fusion.1 = f32[512,8]{1,0:T(8,128)} fusion(f32[8,16384]{0,1:T(8,128)} %bitcast.139, s32[1024]{0:T(1024)S(1)} %pad_clamp_fusion.1), kind=kCustom, calls=%fused_computation.clone | custom fusion | bytes 34816 | tf_op jit(solution)/shard_map/jit(_take)/gather | solution.py:107
  61.9 5.0 %gather_fusion.2 = f32[512,8]{1,0:T(8,128)} fusion(f32[8,16384]{0,1:T(8,128)} %bitcast.140, s32[1024]{0:T(1024)S(1)} %pad_clamp_fusion.1), kind=kCustom, calls=%fused_computation.1.clone | custom fusion | bytes 34816 | tf_op jit(solution)/shard_map/jit(_take)/gather | solution.py:107
  67.8 8.2 %fusion.67 = (f32[8,34,512]{2,1,0:T(8,128)S(1)}, f32[8,34,512]{2,1,0:T(8,128)S(1)}, f32[8,34,512]{2,1,0:T(8,128)S(1)}) fusion(f32[1,8,38,512]{3,2,1,0:T(8,128)S(1)} %bitcast.135, f32[8,36,512]{2,1,0:T(8,128)} %copy-done.2, f32[34,512]{1,0:T(8,128)S(1)} %get-tuple-element.24, f32[34,512]{1,0:T(8,128)S(1)} %get-tuple-element.25, ...), kind=kLoop, calls=%fused_computation.126 | loop fusion | flops 4595712 | bytes 7843840 | tf_op jit(solution)/shard_map/add | solution.py:55
  76.3 3.5 %fusion.94 = (f32[8,32,512]{2,1,0:T(8,128)}, f32[8,32,512]{2,1,0:T(8,128)S(1)}, f32[8,32,512]{2,1,0:T(8,128)S(1)}) fusion(f32[1,8,36,512]{3,2,1,0:T(8,128)S(1)} %bitcast.136, f32[8,34,512]{2,1,0:T(8,128)S(1)} %fusion.62, f32[32,512]{1,0:T(8,128)} %multiply_add_fusion.1, f32[32,512]{1,0:T(8,128)S(1)} %copy-done.10, f32[32,512]{1,0:T(8,128)} %get-tuple-element.61, ...), kind=kLoop, calls=%fused_computation.170 | loop fusion | flops 4325376 | bytes 6881280 | tf_op jit(solution)/shard_map/add | solution.py:58
  80.2 4.7 %copy.31 = f32[8,32,512]{0,2,1:T(8,128)} copy(f32[8,32,512]{2,1,0:T(8,128)S(1)} %get-tuple-element.38) | data formatting | bytes 1048576 | tf_op jit(solution)/shard_map/slice | solution.py:52
  84.9 4.5 %gather_fusion.3 = f32[512,8]{1,0:T(8,128)S(1)} fusion(f32[8,16384]{0,1:T(8,128)} %bitcast.141, s32[1024]{0:T(1024)S(1)} %pad_clamp_fusion.1), kind=kCustom, calls=%fused_computation.2.clone | custom fusion | bytes 34816 | tf_op jit(solution)/shard_map/jit(_take)/gather | solution.py:107
  89.4 4.6 %copy.33 = f32[8,32,512]{0,2,1:T(8,128)} copy(f32[8,32,512]{2,1,0:T(8,128)S(1)} %get-tuple-element.39) | data formatting | bytes 1048576 | tf_op jit(solution)/shard_map/add | solution.py:55
  94.0 4.6 %gather_fusion.4 = f32[512,8]{1,0:T(8,128)S(1)} fusion(f32[8,16384]{0,1:T(8,128)} %bitcast.142, s32[1024]{0:T(1024)S(1)} %pad_clamp_fusion.1), kind=kCustom, calls=%fused_computation.3.clone | custom fusion | bytes 34816 | tf_op jit(solution)/shard_map/jit(_take)/gather | solution.py:107
  100.4 4.2 %collective-permute-start.2 = (bf16[256,512]{0,1:T(8,128)(2,1)S(1)}, bf16[256,512]{0,1:T(8,128)(2,1)S(1)}, u32[]{:S(2)}, u32[]{:S(2)}) collective-permute-start(bf16[256,512]{0,1:T(8,128)(2,1)S(1)} %copy.35), channel_id=1, source_target_pairs={{0,32},{32,64},{64,96},{96,128},{128,160},{160,192},{192,224},{224... | collective-permute-start | bytes 786440 | tf_op jit(solution)/shard_map/ppermute | solution.py:127
  104.6 3.3 %collective-permute-done.2 = bf16[256,512]{0,1:T(8,128)(2,1)S(1)} collective-permute-done((bf16[256,512]{0,1:T(8,128)(2,1)S(1)}, bf16[256,512]{0,1:T(8,128)(2,1)S(1)}, u32[]{:S(2)}, u32[]{:S(2)}) %collective-permute-start.2) | collective-permute-done | bytes 262176 | tf_op jit(solution)/shard_map/ppermute | solution.py:127
  107.9 3.7 %collective-permute-start.3 = (bf16[256,512]{0,1:T(8,128)(2,1)S(1)}, bf16[256,512]{0,1:T(8,128)(2,1)S(1)}, u32[]{:S(2)}, u32[]{:S(2)}) collective-permute-start(bf16[256,512]{0,1:T(8,128)(2,1)S(1)} %collective-permute-done.2), channel_id=1, source_target_pairs={{0,32},{32,64},{64,96},{96,128},{128,160},{160,192},{192,224},{224... | collective-permute-start | bytes 786440 | tf_op jit(solution)/shard_map/ppermute | solution.py:127
  111.6 3.3 %collective-permute-done.3 = bf16[256,512]{0,1:T(8,128)(2,1)S(1)} collective-permute-done((bf16[256,512]{0,1:T(8,128)(2,1)S(1)}, bf16[256,512]{0,1:T(8,128)(2,1)S(1)}, u32[]{:S(2)}, u32[]{:S(2)}) %collective-permute-start.3) | collective-permute-done | bytes 262176 | tf_op jit(solution)/shard_map/ppermute | solution.py:127
  114.9 3.7 %collective-permute-start.4 = (bf16[256,512]{0,1:T(8,128)(2,1)S(1)}, bf16[256,512]{0,1:T(8,128)(2,1)S(1)}, u32[]{:S(2)}, u32[]{:S(2)}) collective-permute-start(bf16[256,512]{0,1:T(8,128)(2,1)S(1)} %collective-permute-done.3), channel_id=1, source_target_pairs={{0,32},{32,64},{64,96},{96,128},{128,160},{160,192},{192,224},{224... | collective-permute-start | bytes 786440 | tf_op jit(solution)/shard_map/ppermute | solution.py:127
  118.6 3.3 %collective-permute-done.4 = bf16[256,512]{0,1:T(8,128)(2,1)S(1)} collective-permute-done((bf16[256,512]{0,1:T(8,128)(2,1)S(1)}, bf16[256,512]{0,1:T(8,128)(2,1)S(1)}, u32[]{:S(2)}, u32[]{:S(2)}) %collective-permute-start.4) | collective-permute-done | bytes 262176 | tf_op jit(solution)/shard_map/ppermute | solution.py:127
  121.9 3.7 %collective-permute-start.5 = (bf16[256,512]{0,1:T(8,128)(2,1)S(1)}, bf16[256,512]{0,1:T(8,128)(2,1)S(1)}, u32[]{:S(2)}, u32[]{:S(2)}) collective-permute-start(bf16[256,512]{0,1:T(8,128)(2,1)S(1)} %collective-permute-done.4), channel_id=1, source_target_pairs={{0,32},{32,64},{64,96},{96,128},{128,160},{160,192},{192,224},{224... | collective-permute-start | bytes 786440 | tf_op jit(solution)/shard_map/ppermute | solution.py:127
  125.6 3.3 %collective-permute-done.5 = bf16[256,512]{0,1:T(8,128)(2,1)S(1)} collective-permute-done((bf16[256,512]{0,1:T(8,128)(2,1)S(1)}, bf16[256,512]{0,1:T(8,128)(2,1)S(1)}, u32[]{:S(2)}, u32[]{:S(2)}) %collective-permute-start.5) | collective-permute-done | bytes 262176 | tf_op jit(solution)/shard_map/ppermute | solution.py:127
  128.9 3.7 %collective-permute-start.6 = (bf16[256,512]{0,1:T(8,128)(2,1)S(1)}, bf16[256,512]{0,1:T(8,128)(2,1)S(1)}, u32[]{:S(2)}, u32[]{:S(2)}) collective-permute-start(bf16[256,512]{0,1:T(8,128)(2,1)S(1)} %collective-permute-done.5), channel_id=1, source_target_pairs={{0,32},{32,64},{64,96},{96,128},{128,160},{160,192},{192,224},{224... | collective-permute-start | bytes 786440 | tf_op jit(solution)/shard_map/ppermute | solution.py:127
  132.6 3.3 %collective-permute-done.6 = bf16[256,512]{0,1:T(8,128)(2,1)S(1)} collective-permute-done((bf16[256,512]{0,1:T(8,128)(2,1)S(1)}, bf16[256,512]{0,1:T(8,128)(2,1)S(1)}, u32[]{:S(2)}, u32[]{:S(2)}) %collective-permute-start.6) | collective-permute-done | bytes 262176 | tf_op jit(solution)/shard_map/ppermute | solution.py:127
  135.9 3.7 %collective-permute-start.7 = (bf16[256,512]{0,1:T(8,128)(2,1)S(1)}, bf16[256,512]{0,1:T(8,128)(2,1)S(1)}, u32[]{:S(2)}, u32[]{:S(2)}) collective-permute-start(bf16[256,512]{0,1:T(8,128)(2,1)S(1)} %collective-permute-done.6), channel_id=1, source_target_pairs={{0,32},{32,64},{64,96},{96,128},{128,160},{160,192},{192,224},{224... | collective-permute-start | bytes 786440 | tf_op jit(solution)/shard_map/ppermute | solution.py:127
  139.6 3.3 %collective-permute-done.7 = bf16[256,512]{0,1:T(8,128)(2,1)S(1)} collective-permute-done((bf16[256,512]{0,1:T(8,128)(2,1)S(1)}, bf16[256,512]{0,1:T(8,128)(2,1)S(1)}, u32[]{:S(2)}, u32[]{:S(2)}) %collective-permute-start.7) | collective-permute-done | bytes 262176 | tf_op jit(solution)/shard_map/ppermute | solution.py:127
  143.0 3.7 %collective-permute-start.8 = (bf16[256,512]{0,1:T(8,128)(2,1)S(1)}, bf16[256,512]{0,1:T(8,128)(2,1)}, u32[]{:S(2)}, u32[]{:S(2)}) collective-permute-start(bf16[256,512]{0,1:T(8,128)(2,1)S(1)} %collective-permute-done.7), channel_id=1, source_target_pairs={{0,32},{32,64},{64,96},{96,128},{128,160},{160,192},{192,224},{224... | collective-permute-start | bytes 786440 | tf_op jit(solution)/shard_map/ppermute | solution.py:127
  150.0 3.8 %collective-permute-start.9 = (bf16[256,512]{0,1:T(8,128)(2,1)}, bf16[256,512]{0,1:T(8,128)(2,1)}, u32[]{:S(2)}, u32[]{:S(2)}) collective-permute-start(bf16[256,512]{0,1:T(8,128)(2,1)} %collective-permute-done.8), channel_id=1, source_target_pairs={{0,32},{32,64},{64,96},{96,128},{128,160},{160,192},{192,224},{224... | collective-permute-start | bytes 786440 | tf_op jit(solution)/shard_map/ppermute | solution.py:127
  155.1 2.3 %collective-permute-done.9 = bf16[256,512]{0,1:T(8,128)(2,1)} collective-permute-done((bf16[256,512]{0,1:T(8,128)(2,1)}, bf16[256,512]{0,1:T(8,128)(2,1)}, u32[]{:S(2)}, u32[]{:S(2)}) %collective-permute-start.9) | collective-permute-done | bytes 262176 | tf_op jit(solution)/shard_map/ppermute | solution.py:127
  159.8 2.3 %collective-permute-done.16 = bf16[256,512]{0,1:T(8,128)(2,1)S(1)} collective-permute-done((bf16[256,512]{0,1:T(8,128)(2,1)S(1)}, bf16[256,512]{0,1:T(8,128)(2,1)S(1)}, u32[]{:S(2)}, u32[]{:S(2)}) %collective-permute-start.16) | collective-permute-done | bytes 262176 | tf_op jit(solution)/shard_map/ppermute | solution.py:129
  164.6 2.5 %constant_dynamic-slice_fusion = bf16[4096,512]{0,1:T(8,128)(2,1)} fusion(bf16[8192,512]{0,1:T(8,128)(2,1)S(1)} %constant_dynamic-update-slice_fusion.5, s32[]{:T(128)S(6)} %select_n.49), kind=kLoop, calls=%fused_computation.276 | loop fusion | bytes 8388612 | tf_op jit(solution)/shard_map/jit(_roll_dynamic)/dynamic_slice | solution.py:131
  167.1 10.2 %gather_fusion = bf16[384,4096]{1,0:T(8,128)(2,1)S(1)} fusion(bf16[4096,512]{0,1:T(8,128)(2,1)} %constant_dynamic-slice_fusion, s32[1024]{0:T(1024)S(1)} %pad_clamp_fusion), kind=kCustom, calls=%fused_computation.4 | custom fusion | bytes 6292992 | tf_op jit(solution)/shard_map/jit(_take)/gather | solution.py:132
  (138 shorter events, 33.6 us)
Async XLA Ops:
  0.7 15.8 %copy-start.18 = (s32[512]{0:T(512)S(1)}, s32[512]{0:T(512)}, u32[]{:S(2)}) copy-start(s32[512]{0:T(512)} %param.25) | copy-start | bytes 6148
  0.7 15.8 %copy-start.21 = (f32[16]{0:T(128)S(1)}, f32[16]{0:T(128)}, u32[]{:S(2)}) copy-start(f32[16]{0:T(128)} %param.23) | copy-start | bytes 196
  3.0 16.6 %collective-permute-start.1 = (f32[36,4,512]{2,1,0:T(4,128)S(1)}, f32[36,4,512]{2,1,0:T(4,128)S(1)}, u32[]{:S(2)}, u32[]{:S(2)}) collective-permute-start(f32[36,4,512]{2,1,0:T(4,128)S(1)} %get-tuple-element.37), channel_id=1, source_target_pairs={{1,0},{2,1},{3,2},{4,3},{5,4},{6,5},{7,6},{8,7},{9,8},{10,9},{11,1... | collective-permute-start | bytes 884744 | tf_op jit(solution)/shard_map/ppermute | solution.py:21
  13.9 11.6 %collective-permute-start = (f32[36,4,512]{2,1,0:T(4,128)S(1)}, f32[36,4,512]{2,1,0:T(4,128)S(1)}, u32[]{:S(2)}, u32[]{:S(2)}) collective-permute-start(f32[36,4,512]{2,1,0:T(4,128)S(1)} %get-tuple-element.36), channel_id=1, source_target_pairs={{0,1},{1,2},{2,3},{3,4},{4,5},{5,6},{6,7},{7,8},{8,9},{9,10},{10,1... | collective-permute-start | bytes 884744 | tf_op jit(solution)/shard_map/ppermute | solution.py:19
  26.0 9.0 %copy-start = (f32[36,40,512]{2,1,0:T(8,128)}, f32[36,40,512]{2,1,0:T(8,128)S(1)}, u32[]{:S(2)}) copy-start(f32[36,40,512]{2,1,0:T(8,128)S(1)} %pad_maximum_fusion) | copy-start | bytes 8847364
  27.6 7.4 %copy-start.8 = (f32[16,40,512]{2,1,0:T(8,128)}, f32[16,40,512]{2,1,0:T(8,128)S(1)}, u32[]{:S(2)}) copy-start(f32[16,40,512]{2,1,0:T(8,128)S(1)} %get-tuple-element.34) | copy-start | bytes 3932164
  41.7 7.3 %copy-start.7 = (f32[16,40,512]{2,1,0:T(8,128)S(1)}, f32[16,40,512]{2,1,0:T(8,128)}, u32[]{:S(2)}) copy-start(f32[16,40,512]{2,1,0:T(8,128)} %get-tuple-element.35) | copy-start | bytes 3932164
  66.9 9.1 %copy-start.1 = (f32[8,36,512]{2,1,0:T(8,128)S(1)}, f32[8,36,512]{2,1,0:T(8,128)}, u32[]{:S(2)}) copy-start(f32[8,36,512]{2,1,0:T(8,128)} %get-tuple-element.15) | copy-start | bytes 1769476
  66.9 9.1 %copy-start.5 = (f32[8,38,512]{2,1,0:T(8,128)S(1)}, f32[8,38,512]{2,1,0:T(8,128)}, u32[]{:S(2)}) copy-start(f32[8,38,512]{2,1,0:T(8,128)} %copy-done.4) | copy-start | bytes 1867780
  67.8 12.1 %copy-start.3 = (f32[8,36,512]{2,1,0:T(8,128)S(1)}, f32[8,36,512]{2,1,0:T(8,128)}, u32[]{:S(2)}) copy-start(f32[8,36,512]{2,1,0:T(8,128)} %copy-done.2) | copy-start | bytes 1769476
  67.8 12.1 %copy-start.14 = (f32[32,512]{1,0:T(8,128)S(1)}, f32[32,512]{1,0:T(8,128)}, u32[]{:S(2)}) copy-start(f32[32,512]{1,0:T(8,128)} %multiply_add_fusion.2) | copy-start | bytes 196612
  80.2 13.8 %copy-start.9 = (f32[8,32,512]{2,1,0:T(8,128)}, f32[8,32,512]{2,1,0:T(8,128)S(1)}, u32[]{:S(2)}) copy-start(f32[8,32,512]{2,1,0:T(8,128)S(1)} %get-tuple-element.39) | copy-start | bytes 1572868
  80.2 18.5 %copy-start.12 = (f32[512,8]{1,0:T(8,128)S(1)}, f32[512,8]{1,0:T(8,128)}, u32[]{:S(2)}) copy-start(f32[512,8]{1,0:T(8,128)} %gather_fusion.1) | copy-start | bytes 49156
  80.2 18.5 %copy-start.13 = (f32[512,8]{1,0:T(8,128)S(1)}, f32[512,8]{1,0:T(8,128)}, u32[]{:S(2)}) copy-start(f32[512,8]{1,0:T(8,128)} %gather_fusion.2) | copy-start | bytes 49156
  84.9 14.3 %copy-start.11 = (f32[8,32,512]{2,1,0:T(8,128)S(1)}, f32[8,32,512]{2,1,0:T(8,128)}, u32[]{:S(2)}) copy-start(f32[8,32,512]{2,1,0:T(8,128)} %param.24) | copy-start | bytes 1572868
  84.9 14.3 %copy-start.19 = (f32[32]{0:T(128)S(1)}, f32[32]{0:T(128)}, u32[]{:S(2)}) copy-start(f32[32]{0:T(128)} %get-tuple-element.66) | copy-start | bytes 388
  84.9 14.3 %copy-start.20 = (f32[32]{0:T(128)S(1)}, f32[32]{0:T(128)}, u32[]{:S(2)}) copy-start(f32[32]{0:T(128)} %get-tuple-element.67) | copy-start | bytes 388
  100.4 7.5 %collective-permute-start.2 = (bf16[256,512]{0,1:T(8,128)(2,1)S(1)}, bf16[256,512]{0,1:T(8,128)(2,1)S(1)}, u32[]{:S(2)}, u32[]{:S(2)}) collective-permute-start(bf16[256,512]{0,1:T(8,128)(2,1)S(1)} %copy.35), channel_id=1, source_target_pairs={{0,32},{32,64},{64,96},{96,128},{128,160},{160,192},{192,224},{224... | collective-permute-start | bytes 786440 | tf_op jit(solution)/shard_map/ppermute | solution.py:127
  107.9 7.0 %collective-permute-start.3 = (bf16[256,512]{0,1:T(8,128)(2,1)S(1)}, bf16[256,512]{0,1:T(8,128)(2,1)S(1)}, u32[]{:S(2)}, u32[]{:S(2)}) collective-permute-start(bf16[256,512]{0,1:T(8,128)(2,1)S(1)} %collective-permute-done.2), channel_id=1, source_target_pairs={{0,32},{32,64},{64,96},{96,128},{128,160},{160,192},{192,224},{224... | collective-permute-start | bytes 786440 | tf_op jit(solution)/shard_map/ppermute | solution.py:127
  111.6 7.0 %collective-permute-start.10 = (bf16[256,512]{0,1:T(8,128)(2,1)S(1)}, bf16[256,512]{0,1:T(8,128)(2,1)S(1)}, u32[]{:S(2)}, u32[]{:S(2)}) collective-permute-start(bf16[256,512]{0,1:T(8,128)(2,1)S(1)} %copy.35), channel_id=1, source_target_pairs={{0,480},{32,0},{64,32},{96,64},{128,96},{160,128},{192,160},{224,1... | collective-permute-start | bytes 786440 | tf_op jit(solution)/shard_map/ppermute | solution.py:129
  114.9 7.0 %collective-permute-start.4 = (bf16[256,512]{0,1:T(8,128)(2,1)S(1)}, bf16[256,512]{0,1:T(8,128)(2,1)S(1)}, u32[]{:S(2)}, u32[]{:S(2)}) collective-permute-start(bf16[256,512]{0,1:T(8,128)(2,1)S(1)} %collective-permute-done.3), channel_id=1, source_target_pairs={{0,32},{32,64},{64,96},{96,128},{128,160},{160,192},{192,224},{224... | collective-permute-start | bytes 786440 | tf_op jit(solution)/shard_map/ppermute | solution.py:127
  118.6 7.0 %collective-permute-start.11 = (bf16[256,512]{0,1:T(8,128)(2,1)S(1)}, bf16[256,512]{0,1:T(8,128)(2,1)S(1)}, u32[]{:S(2)}, u32[]{:S(2)}) collective-permute-start(bf16[256,512]{0,1:T(8,128)(2,1)S(1)} %collective-permute-done.10), channel_id=1, source_target_pairs={{0,480},{32,0},{64,32},{96,64},{128,96},{160,128},{192,160},{224,1... | collective-permute-start | bytes 786440 | tf_op jit(solution)/shard_map/ppermute | solution.py:129
  121.9 7.0 %collective-permute-start.5 = (bf16[256,512]{0,1:T(8,128)(2,1)S(1)}, bf16[256,512]{0,1:T(8,128)(2,1)S(1)}, u32[]{:S(2)}, u32[]{:S(2)}) collective-permute-start(bf16[256,512]{0,1:T(8,128)(2,1)S(1)} %collective-permute-done.4), channel_id=1, source_target_pairs={{0,32},{32,64},{64,96},{96,128},{128,160},{160,192},{192,224},{224... | collective-permute-start | bytes 786440 | tf_op jit(solution)/shard_map/ppermute | solution.py:127
  125.6 7.0 %collective-permute-start.12 = (bf16[256,512]{0,1:T(8,128)(2,1)S(1)}, bf16[256,512]{0,1:T(8,128)(2,1)S(1)}, u32[]{:S(2)}, u32[]{:S(2)}) collective-permute-start(bf16[256,512]{0,1:T(8,128)(2,1)S(1)} %collective-permute-done.11), channel_id=1, source_target_pairs={{0,480},{32,0},{64,32},{96,64},{128,96},{160,128},{192,160},{224,1... | collective-permute-start | bytes 786440 | tf_op jit(solution)/shard_map/ppermute | solution.py:129
  128.9 7.0 %collective-permute-start.6 = (bf16[256,512]{0,1:T(8,128)(2,1)S(1)}, bf16[256,512]{0,1:T(8,128)(2,1)S(1)}, u32[]{:S(2)}, u32[]{:S(2)}) collective-permute-start(bf16[256,512]{0,1:T(8,128)(2,1)S(1)} %collective-permute-done.5), channel_id=1, source_target_pairs={{0,32},{32,64},{64,96},{96,128},{128,160},{160,192},{192,224},{224... | collective-permute-start | bytes 786440 | tf_op jit(solution)/shard_map/ppermute | solution.py:127
  132.6 7.0 %collective-permute-start.13 = (bf16[256,512]{0,1:T(8,128)(2,1)S(1)}, bf16[256,512]{0,1:T(8,128)(2,1)S(1)}, u32[]{:S(2)}, u32[]{:S(2)}) collective-permute-start(bf16[256,512]{0,1:T(8,128)(2,1)S(1)} %collective-permute-done.12), channel_id=1, source_target_pairs={{0,480},{32,0},{64,32},{96,64},{128,96},{160,128},{192,160},{224,1... | collective-permute-start | bytes 786440 | tf_op jit(solution)/shard_map/ppermute | solution.py:129
  135.9 7.0 %collective-permute-start.7 = (bf16[256,512]{0,1:T(8,128)(2,1)S(1)}, bf16[256,512]{0,1:T(8,128)(2,1)S(1)}, u32[]{:S(2)}, u32[]{:S(2)}) collective-permute-start(bf16[256,512]{0,1:T(8,128)(2,1)S(1)} %collective-permute-done.6), channel_id=1, source_target_pairs={{0,32},{32,64},{64,96},{96,128},{128,160},{160,192},{192,224},{224... | collective-permute-start | bytes 786440 | tf_op jit(solution)/shard_map/ppermute | solution.py:127
  139.6 8.4 %collective-permute-start.14 = (bf16[256,512]{0,1:T(8,128)(2,1)S(1)}, bf16[256,512]{0,1:T(8,128)(2,1)S(1)}, u32[]{:S(2)}, u32[]{:S(2)}) collective-permute-start(bf16[256,512]{0,1:T(8,128)(2,1)S(1)} %collective-permute-done.13), channel_id=1, source_target_pairs={{0,480},{32,0},{64,32},{96,64},{128,96},{160,128},{192,160},{224,1... | collective-permute-start | bytes 786440 | tf_op jit(solution)/shard_map/ppermute | solution.py:129
  143.0 7.0 %collective-permute-start.8 = (bf16[256,512]{0,1:T(8,128)(2,1)S(1)}, bf16[256,512]{0,1:T(8,128)(2,1)}, u32[]{:S(2)}, u32[]{:S(2)}) collective-permute-start(bf16[256,512]{0,1:T(8,128)(2,1)S(1)} %collective-permute-done.7), channel_id=1, source_target_pairs={{0,32},{32,64},{64,96},{96,128},{128,160},{160,192},{192,224},{224... | collective-permute-start | bytes 786440 | tf_op jit(solution)/shard_map/ppermute | solution.py:127
  148.1 7.0 %collective-permute-start.15 = (bf16[256,512]{0,1:T(8,128)(2,1)S(1)}, bf16[256,512]{0,1:T(8,128)(2,1)S(1)}, u32[]{:S(2)}, u32[]{:S(2)}) collective-permute-start(bf16[256,512]{0,1:T(8,128)(2,1)S(1)} %collective-permute-done.14), channel_id=1, source_target_pairs={{0,480},{32,0},{64,32},{96,64},{128,96},{160,128},{192,160},{224,1... | collective-permute-start | bytes 786440 | tf_op jit(solution)/shard_map/ppermute | solution.py:129
  150.0 7.4 %collective-permute-start.9 = (bf16[256,512]{0,1:T(8,128)(2,1)}, bf16[256,512]{0,1:T(8,128)(2,1)}, u32[]{:S(2)}, u32[]{:S(2)}) collective-permute-start(bf16[256,512]{0,1:T(8,128)(2,1)} %collective-permute-done.8), channel_id=1, source_target_pairs={{0,32},{32,64},{64,96},{96,128},{128,160},{160,192},{192,224},{224... | collective-permute-start | bytes 786440 | tf_op jit(solution)/shard_map/ppermute | solution.py:127
  155.1 7.0 %collective-permute-start.16 = (bf16[256,512]{0,1:T(8,128)(2,1)S(1)}, bf16[256,512]{0,1:T(8,128)(2,1)S(1)}, u32[]{:S(2)}, u32[]{:S(2)}) collective-permute-start(bf16[256,512]{0,1:T(8,128)(2,1)S(1)} %collective-permute-done.15), channel_id=1, source_target_pairs={{0,480},{32,0},{64,32},{96,64},{128,96},{160,128},{192,160},{224,1... | collective-permute-start | bytes 786440 | tf_op jit(solution)/shard_map/ppermute | solution.py:129
  (7 other events, 20.0 us)
